TPU v7x, 32 devices: a whole 2x2x4 slice. The times are simulated.
32 devices in a mesh: seq: 4 (over x, core), tp: 8 (over z, y).
Axes of the slice: x: 2, y: 2, z: 4, core: 2. Of those that a mesh axis runs over, the one named last changes fastest.
Arguments:
- hidden_in: bfloat16 [2048, 3584], P('seq', 'tp'), may hold values from -6 to 6
- mamba_gain: float32 [3584], replicated, may hold values from 0.1 to 1.9
- w_xz: bfloat16 [2, 1536, 3584], P(None, 'tp'), may hold values from -0.09375 to 0.09375
- w_bc: bfloat16 [3584, 128], replicated, may hold values from -0.09375 to 0.09375
- w_dt: bfloat16 [24, 3584], P('tp'), may hold values from -0.09375 to 0.09375
- dt_bias: float32 [24], P('tp'), may hold values from -2 to 0
- decay_rate: float32 [24], P('tp'), may hold values from 0.00024414062 to 0.3
- conv_x: float32 [4, 1536], P(None, 'tp'), may hold values from -3 to 3
- conv_bc: float32 [4, 128], replicated, may hold values from -3 to 3
- skip_gain: float32 [24], P('tp'), may hold values from 0.5 to 1.5
- inner_gain: float32 [1536], P('tp'), may hold values from 0.1 to 1.9
- w_out: bfloat16 [1536, 3584], P('tp'), may hold values from -0.15625 to 0.15625
- attn_gain: float32 [3584], replicated, may hold values from 0.1 to 1.9
- w_qkv: bfloat16 [3, 1792, 3584], P(None, 'tp'), may hold values from -0.13363062 to 0.13363062
- w_o: bfloat16 [1792, 3584], P('tp'), may hold values from -0.125 to 0.125
- seg_ids: int32 [2048], P('seq'), may hold values from 0 to 3, as said below
- pad_mask: int32 [2048], P('seq'), may hold values from 0 to 1, as said below
- tenant_bounds: int32 [4, 2], replicated, may hold values from 0 to 2048, as said below
Outputs:
- hidden_out: bfloat16 [2048, 3584], P('seq', 'tp')
- kv_cache: bfloat16 [2, 1792, 2048], P(None, 'tp', 'seq')
- tenant_states: float32 [4, 24, 64, 64], P(None, 'tp')
Inputs may be any that keep to these rules, and one draw needn't show every extreme that they name: seg_ids never falls along the tokens; each tenant is one run of at least 128 tokens. `pad_mask`: each tenant's padding is its last tokens, at least one and at most a quarter of its run. `tenant_bounds`: row t holds where tenant t's run in seg_ids starts and one past where it ends; the runs follow one another and cover all 2048 tokens.
All inputs are finite; a program needn't handle non-finite values.
Results may differ from a plain program's by a relative error of at most 0.017.
Values may be sent and summed in bfloat16 or wider, within the bound.
No kernel may reach another device: no remote copies, remote signals or barrier semaphores. Data moves between devices by JAX's collectives and lax.ppermute only.
A program may use at most 128 MiB of HBM per device.

v0:
```python
import jax
import jax.numpy as jnp
from jax import lax
from jax.sharding import PartitionSpec as P

HEADS_DEV = 1
HIGHEST = lax.Precision.HIGHEST


def from_behind(value, axis, by):
    devices = lax.axis_size(axis)
    pairs = [(i, i + by) for i in range(devices) if 0 <= i + by < devices]
    return lax.ppermute(value, axis, pairs)


def rms_scale(rows):
    return lax.rsqrt(jnp.mean(rows * rows, axis=-1, keepdims=True) + 1e-05)


def times_rows(left, weights):
    return lax.dot_general(
        left, weights, (((1,), (1,)), ((), ())), preferred_element_type=jnp.float32
    )


def tenant_of(places, run_starts):
    return jnp.sum((places[:, None] >= run_starts[None, :]).astype(jnp.int32), axis=1) - 1


def row_terms(weights, activations):
    return lax.dot_general(
        weights, activations, (((0,), (1,)), ((), ())), preferred_element_type=jnp.float32
    )


def attend_block(
    carry,
    piece,
    start,
    query_heads,
    query_places,
    query_tenant,
    first_start,
    run_starts,
    head_count,
    score_scale,
):
    key_rows, value_rows, keep_rows = piece
    count = key_rows.shape[0]
    key_heads = key_rows.reshape(count, head_count, -1)
    value_heads = value_rows.reshape(count, head_count, -1)

    def update(state):
        running_max, running_total, running_sum = state
        key_places = jnp.arange(count, dtype=jnp.int32)
        key_tenant = tenant_of(key_places, run_starts)
        visible = (
            (key_tenant[None, :] == query_tenant[:, None])
            & (key_places[None, :] <= query_places[:, None])
            & (keep_rows[None, :] > 0)
        )
        scores = (
            jnp.einsum("qhd,khd->hqk", query_heads, key_heads, preferred_element_type=jnp.float32)
            * score_scale
        )
        scores = jnp.where(visible[None], scores, -1e30)
        fresh_max = jnp.maximum(running_max, jnp.max(scores, axis=-1))
        weights = jnp.exp(scores - fresh_max[..., None]) * visible[None].astype(jnp.float32)
        running_total = jnp.sum(weights, axis=-1)
        running_sum = jnp.einsum(
            "hqk,khd->hqd",
            weights.astype(jnp.bfloat16),
            value_heads,
            preferred_element_type=jnp.float32,
        )
        return (fresh_max, running_total, running_sum)

    wanted = (start <= query_places[-1]) & (start + count - 1 >= first_start)
    return lax.cond(wanted, update, lambda state: state, carry)


def on_device(
    hidden_in,
    mamba_gain,
    w_xz,
    w_bc,
    w_dt,
    dt_bias,
    decay_rate,
    conv_x,
    conv_bc,
    skip_gain,
    inner_gain,
    w_out,
    attn_gain,
    w_qkv,
    w_o,
    seg_ids,
    pad_mask,
    tenant_bounds,
):
    tok_rows = hidden_in.shape[0]
    width = mamba_gain.shape[0]
    tp_count = lax.axis_size("tp")
    seq_base = lax.axis_index("seq") * tok_rows
    places = seq_base + jnp.arange(tok_rows, dtype=jnp.int32)
    run_starts = tenant_bounds[:, 0]
    run_ends = tenant_bounds[:, 1]
    tenant_count = tenant_bounds.shape[0]
    full_in = lax.all_gather(hidden_in, "tp", axis=1, tiled=True)
    wide = full_in.astype(jnp.float32)
    normed = (wide * rms_scale(wide) * mamba_gain).astype(jnp.bfloat16)
    inner_dev = w_xz.shape[1]
    projected = times_rows(normed, w_xz.reshape(2 * inner_dev, width))
    bc_raw = jnp.dot(normed, w_bc, preferred_element_type=jnp.float32)
    live_rows = pad_mask.astype(jnp.float32)
    step_size = jax.nn.softplus(times_rows(normed, w_dt) + dt_bias) * live_rows[:, None]
    raw_input = jnp.concatenate([projected[:, :inner_dev], bc_raw], axis=1)
    conv_kernel = jnp.concatenate([conv_x, conv_bc], axis=1)
    tap_count = conv_kernel.shape[0]
    before = from_behind(raw_input[tok_rows - (tap_count - 1) :], "seq", 1)
    extended = jnp.concatenate([before, raw_input], axis=0)
    before_places = seq_base - (tap_count - 1) + jnp.arange(tap_count - 1, dtype=jnp.int32)
    ext_tenant = jnp.concatenate([tenant_of(before_places, run_starts), seg_ids])
    conv_sum = jnp.zeros_like(raw_input)
    for tap_row in range(tap_count):
        same_tenant = (ext_tenant[tap_row : tap_row + tok_rows] == seg_ids).astype(jnp.float32)
        conv_sum = (
            conv_sum
            + conv_kernel[tap_row] * extended[tap_row : tap_row + tok_rows] * same_tenant[:, None]
        )
    activated = jax.nn.silu(conv_sum)
    state_size = w_bc.shape[1] // 2
    heads_dev = decay_rate.shape[0]
    head_dim = inner_dev // heads_dev
    x_heads = activated[:, :inner_dev].reshape(tok_rows, heads_dev, head_dim)
    input_b = activated[:, inner_dev : inner_dev + state_size]
    output_c = activated[:, inner_dev + state_size :]
    begins = (ext_tenant[tap_count - 2 : tap_count - 2 + tok_rows] != seg_ids).astype(jnp.int32)
    run_label = jnp.cumsum(begins)
    log_total = jnp.cumsum(-step_size * decay_rate, axis=0).T
    row_number = jnp.arange(tok_rows, dtype=jnp.int32)
    lower_same = (row_number[None, :] <= row_number[:, None]) & (
        run_label[:, None] == run_label[None, :]
    )
    log_gap = log_total[:, :, None] - log_total[:, None, :]
    decay_pairs = jnp.where(lower_same[None], jnp.exp(jnp.minimum(log_gap, 0.0)), 0.0)
    c_dot_b = jnp.dot(output_c, input_b.T, precision=HIGHEST)
    mixing = decay_pairs * c_dot_b[None] * step_size.T[:, None, :]
    y_local = jnp.einsum("hij,jhp->ihp", mixing, x_heads, precision=HIGHEST)
    picked = jnp.concatenate(
        [
            jnp.clip(run_ends - 1 - seq_base, 0, tok_rows - 1),
            jnp.full((1,), tok_rows - 1, jnp.int32),
        ]
    )
    owned = ((run_ends - 1 >= seq_base) & (run_ends - 1 < seq_base + tok_rows)).astype(jnp.float32)
    picked_hot = row_number[None, :] == picked[:, None]
    log_picked = jnp.dot(picked_hot.astype(jnp.float32), log_total.T, precision=HIGHEST)
    run_picked = jnp.sum(jnp.where(picked_hot, run_label[None, :], 0), axis=1)
    reaching = (row_number[None, :] <= picked[:, None]) & (
        run_label[None, :] == run_picked[:, None]
    )
    toward = (
        jnp.where(
            reaching[:, None, :],
            jnp.exp(jnp.minimum(log_picked[:, :, None] - log_total[None], 0.0)),
            0.0,
        )
        * step_size.T[None]
    )
    local_states = jnp.einsum("khj,jhp,jn->khpn", toward, x_heads, input_b, precision=HIGHEST)
    carry_factor = jnp.exp(log_picked) * (run_picked == 0).astype(jnp.float32)[:, None]
    block_decay = carry_factor[-1]
    block_state = local_states[-1]
    incoming = jnp.zeros_like(block_state)
    for hop_count in range(lax.axis_size("seq") - 1):
        incoming = from_behind(
            (block_decay[:, None, None] * incoming + block_state).astype(jnp.bfloat16), "seq", 1
        ).astype(jnp.float32)
    entry_factor = jnp.exp(log_total.T) * (run_label == 0).astype(jnp.float32)[:, None]
    y_carry = (
        jnp.einsum("in,hpn->ihp", output_c, incoming, precision=HIGHEST) * entry_factor[:, :, None]
    )
    tenant_part = (carry_factor[:-1, :, None, None] * incoming[None] + local_states[:-1]) * owned[
        :, None, None, None
    ]
    tenant_states = lax.psum(tenant_part.astype(jnp.bfloat16), "seq").astype(jnp.float32)
    y_full = y_local + y_carry + skip_gain[None, :, None] * x_heads
    gated = y_full.reshape(tok_rows, inner_dev) * jax.nn.silu(projected[:, inner_dev:])
    square_sum = lax.psum(jnp.sum(gated * gated, axis=1), "tp")
    inner_scale = lax.rsqrt(square_sum / (inner_dev * tp_count) + 1e-05)
    scaled = (gated * inner_scale[:, None] * inner_gain).astype(jnp.bfloat16)
    my_rows = lax.psum_scatter(
        row_terms(w_out, scaled).astype(jnp.bfloat16), "tp", scatter_dimension=0, tiled=True
    ).astype(jnp.float32)
    mixed_part = (hidden_in.astype(jnp.float32) + my_rows.T).astype(jnp.bfloat16)
    after_mix = lax.all_gather(mixed_part, "tp", axis=1, tiled=True)
    wide_mix = after_mix.astype(jnp.float32)
    normed_attn = (wide_mix * rms_scale(wide_mix) * attn_gain).astype(jnp.bfloat16)
    att_dev = w_qkv.shape[1]
    qkv_rows = times_rows(normed_attn, w_qkv.reshape(3 * att_dev, width)).astype(jnp.bfloat16)
    key_rows = qkv_rows[:, att_dev : 2 * att_dev]
    value_rows = qkv_rows[:, 2 * att_dev :]
    kv_cache = jnp.stack([key_rows.T, value_rows.T])
    head_count = HEADS_DEV
    head_size = att_dev // head_count
    query_heads = qkv_rows[:, :att_dev].reshape(tok_rows, head_count, head_size)
    keep_rows = pad_mask.astype(jnp.bfloat16)
    first_start = jnp.sum(
        jnp.where(jnp.arange(tenant_count, dtype=jnp.int32) == seg_ids[0], run_starts, 0)
    )
    score_scale = head_size ** (-0.5)
    initial = (
        jnp.full((head_count, tok_rows), -1e30, jnp.float32),
        jnp.zeros((head_count, tok_rows), jnp.float32),
        jnp.zeros((head_count, tok_rows, head_size), jnp.float32),
    )
    running_max, running_total, running_sum = attend_block(
        initial,
        (
            lax.all_gather(key_rows, "seq", axis=0, tiled=True),
            lax.all_gather(value_rows, "seq", axis=0, tiled=True),
            lax.all_gather(keep_rows, "seq", axis=0, tiled=True),
        ),
        jnp.int32(0),
        query_heads,
        places,
        seg_ids,
        first_start,
        run_starts,
        head_count,
        score_scale,
    )
    context = (running_sum / running_total[..., None]).astype(jnp.bfloat16)
    context_rows = context.transpose(1, 0, 2).reshape(tok_rows, att_dev)
    attn_part = lax.psum_scatter(
        row_terms(w_o, context_rows).astype(jnp.bfloat16), "tp", scatter_dimension=0, tiled=True
    ).astype(jnp.float32)
    hidden_out = (mixed_part.astype(jnp.float32) + attn_part.T).astype(jnp.bfloat16)
    return (hidden_out, kv_cache, tenant_states)


def solution(mesh):
    return jax.shard_map(
        on_device,
        mesh=mesh,
        in_specs=(
            P("seq", "tp"),
            P(),
            P(None, "tp", None),
            P(),
            P("tp", None),
            P("tp"),
            P("tp"),
            P(None, "tp"),
            P(),
            P("tp"),
            P("tp"),
            P("tp", None),
            P(),
            P(None, "tp", None),
            P("tp", None),
            P("seq"),
            P("seq"),
            P(),
        ),
        out_specs=(P("seq", "tp"), P(None, "tp", "seq"), P(None, "tp", None, None)),
        check_vma=False,
    )
```

profile of v0, /device:TPU:0, one launch (start us, length us, event | category | flops | bytes accessed | tf_op | source)
XLA Modules:
  0.0 445.4 jit_solution(3268128073207426532)
XLA Ops:
  13.4 66.4 %all-gather.4.cloned.1.call-done = bf16[512,3584]{0,1:T(8,128)(2,1)} async-done(((bf16[512,448]{0,1:T(8,128)(2,1)}), bf16[512,3584]{0,1:T(8,128)(2,1)}) %all-gather.4.cloned.1.call-update) | async-done | bytes 3670032 | tf_op jit(solution)/shard_map/all_gather | solution.py:110
  79.8 2.9 fusion.16
  82.7 3.3 negate_multiply_fusion
  87.8 3.9 fusion.99
  98.4 5.3 %collective-permute-start.1 = (bf16[3,64,64]{2,1,0:T(8,128)(2,1)S(1)}, bf16[3,64,64]{2,1,0:T(8,128)(2,1)S(1)}, u32[]{:S(2)}, u32[]{:S(2)}) collective-permute-start(bf16[3,64,64]{2,1,0:T(8,128)(2,1)S(1)} %add_convert_fusion.2), channel_id=1, source_target_pairs={{0,8},{8,16},{16,24},{1,9},{9,17},{17,25},{2,10},{10,18},{18,26},{... | collective-permute-start | bytes 73736 | tf_op jit(solution)/shard_map/ppermute | solution.py:13
  104.7 4.7 %collective-permute-start.2 = (bf16[3,64,64]{2,1,0:T(8,128)(2,1)S(1)}, bf16[3,64,64]{2,1,0:T(8,128)(2,1)S(1)}, u32[]{:S(2)}, u32[]{:S(2)}) collective-permute-start(bf16[3,64,64]{2,1,0:T(8,128)(2,1)S(1)} %add_convert_fusion.1), channel_id=1, source_target_pairs={{0,8},{8,16},{16,24},{1,9},{9,17},{17,25},{2,10},{10,18},{18,26},{... | collective-permute-start | bytes 73736 | tf_op jit(solution)/shard_map/ppermute | solution.py:13
  110.5 4.5 %collective-permute-start.3 = (bf16[3,64,64]{2,1,0:T(8,128)(2,1)S(1)}, bf16[3,64,64]{2,1,0:T(8,128)(2,1)S(1)}, u32[]{:S(2)}, u32[]{:S(2)}) collective-permute-start(bf16[3,64,64]{2,1,0:T(8,128)(2,1)S(1)} %add_convert_fusion), channel_id=1, source_target_pairs={{0,8},{8,16},{16,24},{1,9},{9,17},{17,25},{2,10},{10,18},{18,26},{... | collective-permute-start | bytes 73736 | tf_op jit(solution)/shard_map/ppermute | solution.py:13
  115.1 3.9 fusion.49
  119.5 18.9 %psum.14 = f32[512]{0:T(512)S(1)} all-reduce(f32[512]{0:T(512)S(1)} %get-tuple-element.77), channel_id=1, replica_groups=mesh['seq'=4,'tp'=8] {'tp'}, use_global_device_ids=true, to_apply=%region_8.9 | all-reduce | flops 512 | bytes 4096 | tf_op jit(solution)/shard_map/psum | solution.py:191
  138.4 4.4 fusion.22
  142.8 6.0 %copy.50 = bf16[3584,512]{1,0:T(8,128)(2,1)} copy(bf16[3584,512]{0,1:T(8,128)(2,1)} %fusion.22) | data formatting | bytes 7340032
  149.9 78.3 %reduce-scatter.7.cloned.1.call-done = bf16[448,512]{1,0:T(8,128)(2,1)} async-done(((bf16[3584,512]{1,0:T(8,128)(2,1)}), bf16[448,512]{1,0:T(8,128)(2,1)}) %reduce-scatter.7.cloned.1.call-update) | async-done | bytes 458768
  236.1 5.2 %all-gather = bf16[4,1,512]{2,1,0:T(2,128)(2,1)S(1)} all-gather(bf16[1,1,512]{2,1,0:T(2,128)(2,1)S(1)} %reshape.310), channel_id=1, replica_groups=mesh['seq'=4,'tp'=8] {'seq'}, dimensions={0}, use_global_device_ids=true | all-gather | bytes 5120 | tf_op jit(solution)/shard_map/all_gather | solution.py:224
  243.2 55.9 %all-gather.6.cloned.1.call-done = bf16[512,3584]{0,1:T(8,128)(2,1)} async-done(((bf16[512,448]{0,1:T(8,128)(2,1)}), bf16[512,3584]{0,1:T(8,128)(2,1)}) %all-gather.6.cloned.1.call-update) | async-done | bytes 3670032 | tf_op jit(solution)/shard_map/all_gather | solution.py:198
  299.2 2.9 fusion.19
  302.1 7.1 %fusion.43 = bf16[512,672]{0,1:T(8,128)(2,1)} fusion(bf16[672,3584]{1,0:T(8,128)(2,1)} %bitcast.115, bf16[512,3584]{0,1:T(8,128)(2,1)} %all-gather.6.cloned.1.call-done, f32[3584]{0:T(1024)S(1)} %copy-done.12, f32[512]{0:T(512)S(1)} %add_rsqrt_fusion), kind=kOutput, calls=%fused_computation.52 | convolution fusion | flops 2473934848 | bytes 9191424 | tf_op jit(solution)/shard_map/dot_general | solution.py:21
  311.0 9.7 %all_gather.19 = bf16[2048,224]{0,1:T(8,128)(2,1)} all-gather(bf16[512,224]{0,1:T(8,128)(2,1)S(1)} %get-tuple-element.85), channel_id=1, replica_groups=mesh['seq'=4,'tp'=8] {'seq'}, dimensions={0}, use_global_device_ids=true | all-gather | bytes 1146880 | tf_op jit(solution)/shard_map/all_gather | solution.py:223
  320.7 11.1 %all_gather.18 = bf16[2048,224]{0,1:T(8,128)(2,1)} all-gather(bf16[512,224]{0,1:T(8,128)(2,1)S(1)} %get-tuple-element.86), channel_id=1, replica_groups=mesh['seq'=4,'tp'=8] {'seq'}, dimensions={0}, use_global_device_ids=true | all-gather | bytes 1146880 | tf_op jit(solution)/shard_map/all_gather | solution.py:222
  331.8 10.9 %conditional.1 = (f32[1,512]{1,0:T(1,128)S(1)}, f32[1,512,224]{1,2,0:T(8,128)}) conditional(s32[]{:T(128)} %convert_element_type.146, () %tuple.16, (s32[4,1]{0,1:T(1,128)S(1)}, s32[512]{0:T(512)S(1)}, s32[512]{0:T(512)S(1)}, bf16[4,1,512]{2,1,0:T(2,128)(2,1)S(1)}, bf16[512,672]{0,1:T(8,128)(2,1)}, /*index=5*/bf16[2048,224]{0,1:T(8,128)(2,1)}, ...), branch_computations={%region_12.13_spmd, %region_13.17_spmd} | conditional | flops 965764608 | bytes 20287550 | solution.py:79
  334.2 3.1 fusion.2
  337.4 3.1 fusion.7
  342.7 4.6 %fusion.23 = bf16[3584,512]{0,1:T(8,128)(2,1)} fusion(bf16[224,3584]{1,0:T(8,128)(2,1)} %param.34, f32[1,512,224]{1,2,0:T(8,128)} %get-tuple-element.30, f32[512]{0:T(512)S(1)} %bitcast.107), kind=kOutput, calls=%fused_computation.33 | convolution fusion | flops 824147968 | bytes 5736448 | tf_op jit(solution)/shard_map/dot_general | solution.py:31
  347.3 5.9 %copy.52 = bf16[3584,512]{1,0:T(8,128)(2,1)} copy(bf16[3584,512]{0,1:T(8,128)(2,1)} %fusion.23) | data formatting | bytes 7340032
  356.7 76.2 %reduce-scatter.9.cloned.1.call-done = bf16[448,512]{1,0:T(8,128)(2,1)} async-done(((bf16[3584,512]{1,0:T(8,128)(2,1)}), bf16[448,512]{1,0:T(8,128)(2,1)}) %reduce-scatter.9.cloned.1.call-update) | async-done | bytes 458768
  (117 shorter events, 42.8 us)
Async XLA Ops:
  7.2 80.6 %copy-start = (bf16[2,192,3584]{2,1,0:T(8,128)(2,1)S(1)}, bf16[2,192,3584]{2,1,0:T(8,128)(2,1)}, u32[]{:S(2)}) copy-start(bf16[2,192,3584]{2,1,0:T(8,128)(2,1)} %param.22) | copy-start | bytes 8257540
  7.2 75.5 %copy-start.11 = (f32[3584]{0:T(1024)S(1)}, f32[3584]{0:T(1024)}, u32[]{:S(2)}) copy-start(f32[3584]{0:T(1024)} %param.21) | copy-start | bytes 43012
  7.2 75.5 %copy-start.13 = (f32[3]{0:T(128)S(1)}, f32[3]{0:T(128)}, u32[]{:S(2)}) copy-start(f32[3]{0:T(128)} %param.26) | copy-start | bytes 40
  7.2 75.5 %copy-start.14 = (f32[3]{0:T(128)S(1)}, f32[3]{0:T(128)}, u32[]{:S(2)}) copy-start(f32[3]{0:T(128)} %param.25) | copy-start | bytes 40
  7.2 75.5 %copy-start.10 = (bf16[3,3584]{1,0:T(4,128)(2,1)S(1)}, bf16[3,3584]{1,0:T(4,128)(2,1)}, u32[]{:S(2)}) copy-start(bf16[3,3584]{1,0:T(4,128)(2,1)} %param.24) | copy-start | bytes 64516
  7.2 72.6 %all-gather.4.cloned.1.call-start = ((), (), s32[]{:S(2)}) async-start(), calls=%async_computation.2 | async-start | bytes 4128768 | tf_op jit(solution)/shard_map/all_gather | solution.py:110
  8.0 220.2 %reduce-scatter.7.cloned.1.call-start = ((), (), s32[]{:S(2)}) async-start(), calls=%async_computation.5 | async-start | bytes 4128768
  87.8 3.9 copy-start.1
  87.8 3.9 copy-start.9
  93.3 2.3 collective-permute-start
  98.3 12.1 %copy-start.2 = (f32[5,3,64,64]{3,2,0,1:T(8,128)}, f32[5,3,64,64]{3,2,0,1:T(8,128)S(1)}, u32[]{:S(2)}) copy-start(f32[5,3,64,64]{3,2,0,1:T(8,128)S(1)} %fusion.46) | copy-start | bytes 737284
  98.3 20.7 %copy-start.8 = (f32[3]{0:T(128)S(1)}, f32[3]{0:T(128)}, u32[]{:S(2)}) copy-start(f32[3]{0:T(128)} %param.29) | copy-start | bytes 40
  98.4 6.2 %collective-permute-start.1 = (bf16[3,64,64]{2,1,0:T(8,128)(2,1)S(1)}, bf16[3,64,64]{2,1,0:T(8,128)(2,1)S(1)}, u32[]{:S(2)}, u32[]{:S(2)}) collective-permute-start(bf16[3,64,64]{2,1,0:T(8,128)(2,1)S(1)} %add_convert_fusion.2), channel_id=1, source_target_pairs={{0,8},{8,16},{16,24},{1,9},{9,17},{17,25},{2,10},{10,18},{18,26},{... | collective-permute-start | bytes 73736 | tf_op jit(solution)/shard_map/ppermute | solution.py:13
  104.7 5.7 %collective-permute-start.2 = (bf16[3,64,64]{2,1,0:T(8,128)(2,1)S(1)}, bf16[3,64,64]{2,1,0:T(8,128)(2,1)S(1)}, u32[]{:S(2)}, u32[]{:S(2)}) collective-permute-start(bf16[3,64,64]{2,1,0:T(8,128)(2,1)S(1)} %add_convert_fusion.1), channel_id=1, source_target_pairs={{0,8},{8,16},{16,24},{1,9},{9,17},{17,25},{2,10},{10,18},{18,26},{... | collective-permute-start | bytes 73736 | tf_op jit(solution)/shard_map/ppermute | solution.py:13
  110.5 27.8 %copy-start.6 = (f32[192]{0:T(256)S(1)}, f32[192]{0:T(256)}, u32[]{:S(2)}) copy-start(f32[192]{0:T(256)} %param.30) | copy-start | bytes 2308
  110.5 8.4 %collective-permute-start.3 = (bf16[3,64,64]{2,1,0:T(8,128)(2,1)S(1)}, bf16[3,64,64]{2,1,0:T(8,128)(2,1)S(1)}, u32[]{:S(2)}, u32[]{:S(2)}) collective-permute-start(bf16[3,64,64]{2,1,0:T(8,128)(2,1)S(1)} %add_convert_fusion), channel_id=1, source_target_pairs={{0,8},{8,16},{16,24},{1,9},{9,17},{17,25},{2,10},{10,18},{18,26},{... | collective-permute-start | bytes 73736 | tf_op jit(solution)/shard_map/ppermute | solution.py:13
  142.8 6.1 %copy-start.3 = (bf16[512,448]{0,1:T(8,128)(2,1)S(1)}, bf16[512,448]{0,1:T(8,128)(2,1)}, u32[]{:S(2)}) copy-start(bf16[512,448]{0,1:T(8,128)(2,1)} %param.20) | copy-start | bytes 1376260
  148.7 83.8 %copy-start.5 = (s32[512]{0:T(512)S(1)}, s32[512]{0:T(512)}, u32[]{:S(2)}) copy-start(s32[512]{0:T(512)} %param.35) | copy-start | bytes 6148
  148.7 84.9 %copy-start.7 = (s32[4,2]{0,1:T(2,128)S(1)}, s32[4,2]{0,1:T(2,128)}, u32[]{:S(2)}) copy-start(s32[4,2]{0,1:T(2,128)} %param.37) | copy-start | bytes 100
  148.8 150.4 %all-gather.6.cloned.1.call-start = ((), (), s32[]{:S(2)}) async-start(), calls=%async_computation.3 | async-start | bytes 4128768 | tf_op jit(solution)/shard_map/all_gather | solution.py:198
  149.9 152.2 %copy-start.12 = (f32[3584]{0:T(1024)S(1)}, f32[3584]{0:T(1024)}, u32[]{:S(2)}) copy-start(f32[3584]{0:T(1024)} %param.32) | copy-start | bytes 43012
  232.5 120.8 %all-reduce.2.cloned.1.call-start = ((), (), s32[]{:S(2)}) async-start(), calls=%async_computation.4 | async-start | bytes 393216 | tf_op jit(solution)/shard_map/psum | solution.py:188
  243.2 189.7 %reduce-scatter.9.cloned.1.call-start = ((), (), s32[]{:S(2)}) async-start(), calls=%async_computation.6 | async-start | bytes 4128768
  334.2 3.1 copy-start.4
Sparse Core Ops, SparseCore 0:
  10.2 69.5 all-gather.3
  148.9 79.2 reduce-scatter.6
  232.6 66.5 all-gather.5
  301.9 30.5 all-reduce.1
  353.4 79.4 reduce-scatter.8
where the time goes:
time: 447 us; the launch traced here: 445 us
  waiting for transfers between devices  279 us (62%)
  blocking collectives  44.9 us (10%)
  matrix products  38 us (9%)
  local copies, waits for them, and re-layouts  27.5 us (6%)
  other arithmetic  24.2 us (5%)
  starting transfers between devices  16 us (4%)
  between operations  15.4 us (3%)
    unnamed x7, waiting for transfers between devices  155 us
    all_gather x1, waiting for transfers between devices, on_device(): full_in = lax.all_gather(hidden_in, 'tp', axis=1, tiled=True)  66.4 us
    all_gather x1, waiting for transfers between devices, on_device(): after_mix = lax.all_gather(mixed_part, 'tp', axis=1, tiled=True)  55.9 us
    unnamed x37, local copies, waits for them, and re-layouts  20.7 us
    psum x1, blocking collectives, on_device(): square_sum = lax.psum(jnp.sum(gated * gated, axis=1), 'tp')  18.9 us
    ppermute x4, starting transfers between devices, from_behind(): return lax.ppermute(value, axis, pairs)  15.8 us
    dot_general x3, matrix products, times_rows(): lax.dot_general(left, weights, (((1,), (1,)), ((), ())), preferred_elemen...  14.3 us
    all_gather x1, blocking collectives, on_device(): lax.all_gather(key_rows, 'seq', axis=0, tiled=True)  11.1 us
  transfers between devices with their start and end apart: 9, of which 6 were waited for; matrix products, arithmetic and copies ran while one was open for 12% of the time, Pallas kernels for 0%

commit v1 on v0

--- a/solution.py
+++ b/solution.py
@@ -1,3 +1,4 @@
+import functools
 import jax
 import jax.numpy as jnp
 from jax import lax
@@ -5,6 +6,28 @@
 
 HEADS_DEV = 1
 HIGHEST = lax.Precision.HIGHEST
+
+
+def turn_frame(view, on_dim):
+    nd = lax.psum(1, "seq")
+    blocks_here = [(k, (k + 1) % nd) for k in range(nd)]
+    pieces_in = [(k, (k - 1) % nd) for k in range(nd)]
+    q_next, prior = ([view], [view])
+    for _ in range(nd // 2):
+        block_now = lax.ppermute(q_next[-1], "seq", blocks_here)
+        q_next.append(block_now)
+    s = 0
+    while s < (nd - 1) // 2:
+        low = lax.ppermute(prior[-1], axis_name="seq", perm=pieces_in)
+        prior.append(low)
+        s += 1
+    x_now = jnp.concatenate([*q_next[::-1], *prior[1:]], on_dim)
+    item_now = lax.axis_index("seq")
+    w_next = jnp.roll(x_now, (item_now - nd // 2) * view.shape[on_dim], on_dim)
+    return w_next
+
+
+form_the_views = functools.partial(turn_frame, on_dim=0)
 
 
 def from_behind(value, axis, by):
@@ -220,7 +243,7 @@
         initial,
         (
             lax.all_gather(key_rows, "seq", axis=0, tiled=True),
-            lax.all_gather(value_rows, "seq", axis=0, tiled=True),
+            form_the_views(value_rows),
             lax.all_gather(keep_rows, "seq", axis=0, tiled=True),
         ),
         jnp.int32(0),

time: 447 us -> 466 us (1.043)
  local copies, waits for them, and re-layouts: 27.5 us -> 44.8 us
  blocking collectives: 44.9 us -> 34.6 us
  waiting for transfers between devices: 279 us -> 287 us
    unnamed x37 -> x61, local copies, waits for them, and re-layouts: 20.7 us -> 31.2 us
    all_gather x1 -> x0, blocking collectives: 9.73 us -> none  [on_device(): lax.all_gather(value_rows, 'seq', axis=0, tiled=True)]
    all_gather x1, waiting for transfers between devices: 55.9 us -> 64.2 us  [on_device(): after_mix = lax.all_gather(mixed_part, 'tp', axis=1, tiled=True)]
  transfers between devices with their start and end apart: 9 -> 12, of which waited for: 6 -> 7; matrix products, arithmetic and copies ran while one was open for 12% -> 14% of each run, Pallas kernels for 0% -> 0%
where the time goes in v1:
time: 466 us; the launch traced here: 465 us
  waiting for transfers between devices  287 us (62%)
  local copies, waits for them, and re-layouts  44.8 us (10%)
  matrix products  38 us (8%)
  blocking collectives  34.6 us (7%)
  other arithmetic  26.8 us (6%)
  starting transfers between devices  17.9 us (4%)
  between operations  15.5 us (3%)
    unnamed x7, waiting for transfers between devices  154 us
    all_gather x1, waiting for transfers between devices, on_device(): full_in = lax.all_gather(hidden_in, 'tp', axis=1, tiled=True)  65.3 us
    all_gather x1, waiting for transfers between devices, on_device(): after_mix = lax.all_gather(mixed_part, 'tp', axis=1, tiled=True)  64.2 us
    unnamed x61, local copies, waits for them, and re-layouts  31.2 us
    psum x1, blocking collectives, on_device(): square_sum = lax.psum(jnp.sum(gated * gated, axis=1), 'tp')  18.9 us
    ppermute x4, starting transfers between devices, from_behind(): return lax.ppermute(value, axis, pairs)  15.8 us
    dot_general x3, matrix products, times_rows(): lax.dot_general(left, weights, (((1,), (1,)), ((), ())), preferred_elemen...  9.95 us
  transfers between devices with their start and end apart: 12, of which 7 were waited for; matrix products, arithmetic and copies ran while one was open for 14% of the time, Pallas kernels for 0%

profile of v1, /device:TPU:0, one launch (start us, length us, event | category | flops | bytes accessed | tf_op | source)
XLA Modules:
  0.0 465.0 jit_solution(6031305998338953485)
XLA Ops:
  14.4 65.3 %all-gather.4.cloned.1.call-done = bf16[512,3584]{0,1:T(8,128)(2,1)} async-done(((bf16[512,448]{0,1:T(8,128)(2,1)}), bf16[512,3584]{0,1:T(8,128)(2,1)}) %all-gather.4.cloned.1.call-update) | async-done | bytes 3670032 | tf_op jit(solution)/shard_map/all_gather | solution.py:133
  79.8 3.0 fusion.18
  85.5 3.9 fusion.101
  96.1 5.3 %collective-permute-start.1 = (bf16[3,64,64]{2,1,0:T(8,128)(2,1)S(1)}, bf16[3,64,64]{2,1,0:T(8,128)(2,1)S(1)}, u32[]{:S(2)}, u32[]{:S(2)}) collective-permute-start(bf16[3,64,64]{2,1,0:T(8,128)(2,1)S(1)} %add_convert_fusion.2), channel_id=1, source_target_pairs={{0,8},{8,16},{16,24},{1,9},{9,17},{17,25},{2,10},{10,18},{18,26},{... | collective-permute-start | bytes 73736 | tf_op jit(solution)/shard_map/ppermute | solution.py:36
  102.4 4.7 %collective-permute-start.2 = (bf16[3,64,64]{2,1,0:T(8,128)(2,1)S(1)}, bf16[3,64,64]{2,1,0:T(8,128)(2,1)S(1)}, u32[]{:S(2)}, u32[]{:S(2)}) collective-permute-start(bf16[3,64,64]{2,1,0:T(8,128)(2,1)S(1)} %add_convert_fusion.1), channel_id=1, source_target_pairs={{0,8},{8,16},{16,24},{1,9},{9,17},{17,25},{2,10},{10,18},{18,26},{... | collective-permute-start | bytes 73736 | tf_op jit(solution)/shard_map/ppermute | solution.py:36
  108.2 4.5 collective-permute-start.3
  112.7 3.9 fusion.51
  117.2 18.9 %psum.14 = f32[512]{0:T(512)S(1)} all-reduce(f32[512]{0:T(512)S(1)} %get-tuple-element.210), channel_id=1, replica_groups=mesh['seq'=4,'tp'=8] {'tp'}, use_global_device_ids=true, to_apply=%region_8.9 | all-reduce | flops 512 | bytes 4096 | tf_op jit(solution)/shard_map/psum | solution.py:214
  136.0 4.4 fusion.24
  140.5 5.9 %copy.49 = bf16[3584,512]{1,0:T(8,128)(2,1)} copy(bf16[3584,512]{0,1:T(8,128)(2,1)} %fusion.24) | data formatting | bytes 7340032
  148.4 77.4 %reduce-scatter.7.cloned.1.call-done = bf16[448,512]{1,0:T(8,128)(2,1)} async-done(((bf16[3584,512]{1,0:T(8,128)(2,1)}), bf16[448,512]{1,0:T(8,128)(2,1)}) %reduce-scatter.7.cloned.1.call-update) | async-done | bytes 458768
  232.6 64.2 %all-gather.6.cloned.1.call-done = bf16[512,3584]{0,1:T(8,128)(2,1)} async-done(((bf16[512,448]{0,1:T(8,128)(2,1)}), bf16[512,3584]{0,1:T(8,128)(2,1)}) %all-gather.6.cloned.1.call-update) | async-done | bytes 3670032 | tf_op jit(solution)/shard_map/all_gather | solution.py:221
  296.8 3.0 fusion.21
  299.9 5.1 %fusion.45 = bf16[512,672]{0,1:T(8,128)(2,1)S(1)} fusion(bf16[672,3584]{1,0:T(8,128)(2,1)} %bitcast.114, bf16[512,3584]{0,1:T(8,128)(2,1)S(1)} %copy-done.5, f32[3584]{0:T(1024)S(1)} %copy-done.21, f32[512]{0:T(512)S(1)} %add_rsqrt_fusion), kind=kOutput, calls=%fused_computation.54 | convolution fusion | flops 2473934848 | bytes 9191424 | tf_op jit(solution)/shard_map/dot_general | solution.py:44
  311.0 6.5 %all-gather = bf16[4,1,512]{2,1,0:T(2,128)(2,1)} all-gather(bf16[1,1,512]{2,1,0:T(2,128)(2,1)} %reshape.328), channel_id=1, replica_groups=mesh['seq'=4,'tp'=8] {'seq'}, dimensions={0}, use_global_device_ids=true | all-gather | bytes 5120 | tf_op jit(solution)/shard_map/all_gather | solution.py:247
  333.0 9.3 %all_gather.15 = bf16[2048,224]{0,1:T(8,128)(2,1)} all-gather(bf16[512,224]{0,1:T(8,128)(2,1)S(1)} %get-tuple-element.219), channel_id=1, replica_groups=mesh['seq'=4,'tp'=8] {'seq'}, dimensions={0}, use_global_device_ids=true | all-gather | bytes 1146880 | tf_op jit(solution)/shard_map/all_gather | solution.py:245
  343.1 19.5 %conditional.1 = (f32[1,512]{1,0:T(1,128)S(1)}, f32[1,512,224]{1,2,0:T(8,128)}) conditional(s32[]{:T(128)} %convert_element_type.152, () %tuple.27, (s32[4,1]{0,1:T(1,128)S(1)}, s32[512]{0:T(512)S(1)}, s32[512]{0:T(512)S(1)}, bf16[4,1,512]{2,1,0:T(2,128)(2,1)S(1)}, bf16[512,672]{0,1:T(8,128)(2,1)}, /*index=5*/bf16[2048,224]{0,1:T(8,128)(2,1)}, ...), branch_computations={%region_12.13_spmd, %region_13.17_spmd} | conditional | flops 965764608 | bytes 37195992 | solution.py:102
  345.7 4.8 %fusion.2 = (f32[512]{0:T(512)S(1)}, f32[512,2048]{1,0:T(8,128)}) fusion(pred[2048]{0:T(1024)(128)(4,1)S(1)} %broadcast_compare_fusion, s32[512]{0:T(512)S(1)} %get-tuple-element.123, s32[512]{0:T(512)S(1)} %get-tuple-element.122, s32[2048]{0:T(1024)S(1)} %broadcast_add_fusion, bf16[2048,224]{0,1:T(8,128)(2,1)} %get-tuple-element.193, bf16[512,672]{1,0:T(8,128)(2,1)} %copy.42), kind=kOutput, calls=%fused_computation.5 | convolution fusion | flops 477101568 | bytes 5390336 | tf_op jit(solution)/shard_map/cond/branch_1_fun/qhd,khd->hqk/dot_general | solution.py:86
  350.6 4.0 copy.44
  354.5 5.7 %fusion.7 = f32[1,512,224]{1,2,0:T(8,128)} fusion(f32[512,2048]{1,0:T(8,128)} %get-tuple-element.215, f32[512]{0:T(512)S(1)} %broadcast_maximum_fusion, bf16[4096,224]{1,0:T(8,128)(2,1)} %copy.44, s32[]{:T(128)S(6)} %select_n.44, s32[512]{0:T(512)S(1)} %get-tuple-element.123, s32[2048]{0:T(1024)S(1)} %broadcast_add_fusion, s32[512]{0:T(512)S(1)} %get-tuple-element.122, ...), kind=kOutput, calls=%fused_computation.9 | convolution fusion | flops 479199232 | bytes 5718020 | tf_op jit(solution)/shard_map/cond/branch_1_fun/hqk,khd->hqd/dot_general | solution.py:93
  360.3 2.3 fusion.4
  362.5 4.6 fusion.25
  367.1 5.9 %copy.51 = bf16[3584,512]{1,0:T(8,128)(2,1)} copy(bf16[3584,512]{0,1:T(8,128)(2,1)} %fusion.25) | data formatting | bytes 7340032
  376.5 75.9 %reduce-scatter.9.cloned.1.call-done = bf16[448,512]{1,0:T(8,128)(2,1)} async-done(((bf16[3584,512]{1,0:T(8,128)(2,1)}), bf16[448,512]{1,0:T(8,128)(2,1)}) %reduce-scatter.9.cloned.1.call-update) | async-done | bytes 458768
  (149 shorter events, 60.7 us)
Async XLA Ops:
  7.2 78.3 %copy-start = (bf16[2,192,3584]{2,1,0:T(8,128)(2,1)S(1)}, bf16[2,192,3584]{2,1,0:T(8,128)(2,1)}, u32[]{:S(2)}) copy-start(bf16[2,192,3584]{2,1,0:T(8,128)(2,1)} %param.22) | copy-start | bytes 8257540
  7.2 75.7 %copy-start.20 = (f32[3584]{0:T(1024)S(1)}, f32[3584]{0:T(1024)}, u32[]{:S(2)}) copy-start(f32[3584]{0:T(1024)} %param.21) | copy-start | bytes 43012
  7.2 75.6 %copy-start.19 = (bf16[3,3584]{1,0:T(4,128)(2,1)S(1)}, bf16[3,3584]{1,0:T(4,128)(2,1)}, u32[]{:S(2)}) copy-start(bf16[3,3584]{1,0:T(4,128)(2,1)} %param.24) | copy-start | bytes 64516
  7.2 75.6 %copy-start.23 = (f32[3]{0:T(128)S(1)}, f32[3]{0:T(128)}, u32[]{:S(2)}) copy-start(f32[3]{0:T(128)} %param.25) | copy-start | bytes 40
  7.2 75.6 %copy-start.22 = (f32[3]{0:T(128)S(1)}, f32[3]{0:T(128)}, u32[]{:S(2)}) copy-start(f32[3]{0:T(128)} %param.26) | copy-start | bytes 40
  7.2 72.6 %all-gather.4.cloned.1.call-start = ((), (), s32[]{:S(2)}) async-start(), calls=%async_computation.2 | async-start | bytes 4128768 | tf_op jit(solution)/shard_map/all_gather | solution.py:133
  8.0 217.8 %reduce-scatter.7.cloned.1.call-start = ((), (), s32[]{:S(2)}) async-start(), calls=%async_computation.5 | async-start | bytes 4128768
  91.0 2.3 collective-permute-start
  96.1 6.2 %collective-permute-start.1 = (bf16[3,64,64]{2,1,0:T(8,128)(2,1)S(1)}, bf16[3,64,64]{2,1,0:T(8,128)(2,1)S(1)}, u32[]{:S(2)}, u32[]{:S(2)}) collective-permute-start(bf16[3,64,64]{2,1,0:T(8,128)(2,1)S(1)} %add_convert_fusion.2), channel_id=1, source_target_pairs={{0,8},{8,16},{16,24},{1,9},{9,17},{17,25},{2,10},{10,18},{18,26},{... | collective-permute-start | bytes 73736 | tf_op jit(solution)/shard_map/ppermute | solution.py:36
  102.4 5.7 %collective-permute-start.2 = (bf16[3,64,64]{2,1,0:T(8,128)(2,1)S(1)}, bf16[3,64,64]{2,1,0:T(8,128)(2,1)S(1)}, u32[]{:S(2)}, u32[]{:S(2)}) collective-permute-start(bf16[3,64,64]{2,1,0:T(8,128)(2,1)S(1)} %add_convert_fusion.1), channel_id=1, source_target_pairs={{0,8},{8,16},{16,24},{1,9},{9,17},{17,25},{2,10},{10,18},{18,26},{... | collective-permute-start | bytes 73736 | tf_op jit(solution)/shard_map/ppermute | solution.py:36
  108.2 27.8 %copy-start.14 = (f32[192]{0:T(256)S(1)}, f32[192]{0:T(256)}, u32[]{:S(2)}) copy-start(f32[192]{0:T(256)} %param.30) | copy-start | bytes 2308
  108.2 8.4 %collective-permute-start.3 = (bf16[3,64,64]{2,1,0:T(8,128)(2,1)S(1)}, bf16[3,64,64]{2,1,0:T(8,128)(2,1)S(1)}, u32[]{:S(2)}, u32[]{:S(2)}) collective-permute-start(bf16[3,64,64]{2,1,0:T(8,128)(2,1)S(1)} %add_convert_fusion), channel_id=1, source_target_pairs={{0,8},{8,16},{16,24},{1,9},{9,17},{17,25},{2,10},{10,18},{18,26},{... | collective-permute-start | bytes 73736 | tf_op jit(solution)/shard_map/ppermute | solution.py:36
  146.4 85.0 %copy-start.15 = (s32[4,2]{0,1:T(2,128)S(1)}, s32[4,2]{0,1:T(2,128)}, u32[]{:S(2)}) copy-start(s32[4,2]{0,1:T(2,128)} %param.37) | copy-start | bytes 100
  146.4 150.4 %all-gather.6.cloned.1.call-start = ((), (), s32[]{:S(2)}) async-start(), calls=%async_computation.3 | async-start | bytes 4128768 | tf_op jit(solution)/shard_map/all_gather | solution.py:221
  148.4 151.4 %copy-start.21 = (f32[3584]{0:T(1024)S(1)}, f32[3584]{0:T(1024)}, u32[]{:S(2)}) copy-start(f32[3584]{0:T(1024)} %param.32) | copy-start | bytes 43012
  230.1 143.0 %all-reduce.2.cloned.1.call-start = ((), (), s32[]{:S(2)}) async-start(), calls=%async_computation.4 | async-start | bytes 393216 | tf_op jit(solution)/shard_map/psum | solution.py:211
  306.6 11.7 %collective-permute-start.4 = (bf16[512,224]{0,1:T(8,128)(2,1)}, bf16[512,224]{0,1:T(8,128)(2,1)S(1)}, u32[]{:S(2)}, u32[]{:S(2)}) collective-permute-start(bf16[512,224]{0,1:T(8,128)(2,1)} %slice.149), channel_id=1, source_target_pairs={{0,8},{8,16},{16,24},{24,0},{1,9},{9,17},{17,25},{25,1},{2,10},{10... | collective-permute-start | bytes 688136 | tf_op jit(solution)/shard_map/ppermute | solution.py:17
  318.2 24.8 %copy-start.10 = (bf16[4,1,512]{2,1,0:T(2,128)(2,1)S(1)}, bf16[4,1,512]{2,1,0:T(2,128)(2,1)}, u32[]{:S(2)}) copy-start(bf16[4,1,512]{2,1,0:T(2,128)(2,1)} %all-gather) | copy-start | bytes 12292
  318.2 24.8 %copy-start.11 = (s32[512]{0:T(512)S(1)}, s32[512]{0:T(512)}, u32[]{:S(2)}) copy-start(s32[512]{0:T(512)} %param.35) | copy-start | bytes 6148
  318.2 24.8 %copy-start.13 = (s32[512]{0:T(512)S(1)}, s32[512]{0:T(512)}, u32[]{:S(2)}) copy-start(s32[512]{0:T(512)} %iota_add_fusion) | copy-start | bytes 6148
  318.3 24.8 %copy-start.16 = (s32[4,1]{0,1:T(1,128)S(1)}, s32[4,1]{0,1:T(1,128)}, u32[]{:S(2)}) copy-start(s32[4,1]{0,1:T(1,128)} %get-tuple-element.228) | copy-start | bytes 52
  318.3 5.6 %collective-permute-start.5 = (bf16[512,224]{0,1:T(8,128)(2,1)S(1)}, bf16[512,224]{0,1:T(8,128)(2,1)}, u32[]{:S(2)}, u32[]{:S(2)}) collective-permute-start(bf16[512,224]{0,1:T(8,128)(2,1)S(1)} %collective-permute-done.4), channel_id=1, source_target_pairs={{0,8},{8,16},{16,24},{24,0},{1,9},{9,17},{17,25},{25,1},{2,10},{10... | collective-permute-start | bytes 688136 | tf_op jit(solution)/shard_map/ppermute | solution.py:17
  320.5 132.0 %reduce-scatter.9.cloned.1.call-start = ((), (), s32[]{:S(2)}) async-start(), calls=%async_computation.6 | async-start | bytes 4128768
  320.5 7.5 %collective-permute-start.6 = (bf16[512,224]{0,1:T(8,128)(2,1)}, bf16[512,224]{0,1:T(8,128)(2,1)S(1)}, u32[]{:S(2)}, u32[]{:S(2)}) collective-permute-start(bf16[512,224]{0,1:T(8,128)(2,1)} %slice.149), channel_id=1, source_target_pairs={{0,24},{8,0},{16,8},{24,16},{1,25},{9,1},{17,9},{25,17},{2,26},{10... | collective-permute-start | bytes 688136 | tf_op jit(solution)/shard_map/ppermute | solution.py:21
  (12 other events, 97.1 us)
Sparse Core Ops, SparseCore 0:
  10.2 69.5 all-gather.3
  146.5 79.2 reduce-scatter.6
  230.2 66.4 all-gather.5
  320.6 30.1 all-reduce.1
  373.2 79.2 reduce-scatter.8
